TPU v7x, 512 devices: a whole 4x4x16 slice. The times are simulated.
512 devices in a mesh: frow: 16 (over z_lo, y), fcol: 32 (over z_hi, x, core).
Axes of the slice: x: 4, y: 4, z: 16 (z_hi: 4, z_lo: 4; z = z_hi * 4 + z_lo), core: 2. Of those that a mesh axis runs over, the one named last changes fastest.
Arguments:
- vis: float32 [2, 131072], P(None, ('frow', 'fcol')), may hold values from -6 to 6
- station_pairs: int32 [2, 131072], P(None, ('frow', 'fcol')), may hold values from 0 to 511
- visibility_time_slot: int32 [131072], P(('frow', 'fcol')), may hold values from 0 to 15
- station_u_cells: int32 [512], replicated, may hold values from -4096 to 4095
- station_v_cells: int32 [512], replicated, may hold values from -4096 to 4095
- facet_station_gains: float32 [16, 32, 2, 8192], P('frow', 'fcol'), may hold values from -6 to 6
- holder_device_order: int32 [512], replicated, may hold values from 0 to 511, each once
Outputs:
- image: float32 [16384, 16384], P('frow', 'fcol')
Inputs may be any that keep to these rules, and one draw needn't show every extreme that they name: `holder_device_order`: a permutation; its first 4 entries name distinct devices.
All inputs are finite; a program needn't handle non-finite values.
Results may differ from a plain program's by a relative error of at most 0.0037.
Values sent between devices are 32-bit elements; how exact they have to be, the bound alone decides.
A program may use at most 64 MiB of HBM per device.

v0:
```python
import math
import jax
import jax.numpy as jnp
from jax import lax
from jax.sharding import PartitionSpec as P

R = 1024
C = 512
M = 64
NT = 16
NBLK = 4


def extended_2(x, sides, width):
    for axis, dim in sides:
        size, length = (lax.axis_size(axis), x.shape[dim])
        up = [(i, (i + 1) % size) for i in range(size - 1)]
        down = [(j, i) for i, j in up]
        last = lax.slice_in_dim(x, length - width, length, axis=dim)
        leading = lax.slice_in_dim(x, 0, width, axis=dim)
        before = lax.ppermute(last, axis, up)
        after = lax.ppermute(leading, axis, down)
        x = jnp.concatenate([before, x, after], axis=dim)
    return x


def broadcast(value, axis, source):
    kept = jnp.where(lax.axis_index(axis) == source, value, 0).astype(value.dtype)
    return lax.psum(kept, axis)


def taper_line(length):
    index = jnp.arange(length + 2 * M, dtype=jnp.int32).astype(jnp.float32)
    rising = (index + 0.5) / (2.0 * M)
    falling = (length + 2 * M - index - 0.5) / (2.0 * M)
    return jnp.minimum(jnp.minimum(rising, falling), 1.0)


def phase_angles(freq, pixels, modulus):
    cells = jnp.mod(freq, modulus)[None, :] * jnp.mod(pixels, modulus)[:, None] % modulus
    return cells.astype(jnp.float32) * (2.0 * math.pi / modulus)


def block_weights(values, label_names, g_tab, scale):
    first = label_names[0] * NT + label_names[2]
    second = label_names[1] * NT + label_names[2]
    g1r = g_tab[0][first]
    g1i = g_tab[1][first]
    g2r = g_tab[0][second]
    g2i = g_tab[1][second]
    real_gain = g1r * g2r + g1i * g2i
    imag_gain = g1i * g2r - g1r * g2i
    wreal = scale * (values[0] * real_gain - values[1] * imag_gain)
    wimag = scale * (values[0] * imag_gain + values[1] * real_gain)
    return (wreal, wimag)


def fold_columns(field):
    edges = jnp.concatenate([field[:, :M], field[:, -M:]], 1)
    extended = extended_2(edges, (("fcol", 1),), M)
    inner = field[:, M:-M]
    return jnp.concatenate(
        [inner[:, :M] + extended[:, :M], inner[:, M:-M], inner[:, -M:] + extended[:, -M:]], 1
    )


def fold_rows(field):
    edges = jnp.concatenate([field[:M], field[-M:]], 0)
    extended = extended_2(edges, (("frow", 0),), M)
    inner = field[M:-M]
    return jnp.concatenate([inner[:M] + extended[:M], inner[M:-M], inner[-M:] + extended[-M:]], 0)


def shards(
    vis,
    station_pairs,
    visibility_time_slot,
    station_u_cells,
    station_v_cells,
    facet_station_gains,
    holder_device_order,
):
    count_rows = lax.axis_size("frow")
    count_cols = lax.axis_size("fcol")
    n_rows = R * count_rows
    n_cols = C * count_cols
    frow_at = lax.axis_index("frow")
    fcol_at = lax.axis_index("fcol")
    g_tab = facet_station_gains[0, 0]
    label_names = jnp.concatenate([station_pairs, visibility_time_slot[None, :]], 0)
    block_size = vis.shape[1]
    scale = 0.5 / math.sqrt(NBLK * block_size)
    rows = frow_at * R - M + jnp.arange(R + 2 * M, dtype=jnp.int32)
    cols = fcol_at * C - M + jnp.arange(C + 2 * M, dtype=jnp.int32)
    total = jnp.zeros((R + 2 * M, C + 2 * M), jnp.float32)
    for step in range(NBLK):
        owner = holder_device_order[step]
        values, tag_names = (
            broadcast(vis, ("frow", "fcol"), owner),
            broadcast(label_names, ("frow", "fcol"), owner),
        )
        wreal, wimag = block_weights(values, tag_names, g_tab, scale)
        frequency_u = station_u_cells[tag_names[0]] - station_u_cells[tag_names[1]]
        frequency_v = station_v_cells[tag_names[0]] - station_v_cells[tag_names[1]]
        theta = phase_angles(frequency_u, rows, n_rows)
        phi = phase_angles(frequency_v, cols, n_cols).T
        row_table = jnp.concatenate([jnp.cos(theta), jnp.sin(theta)], 1).astype(jnp.bfloat16)
        top = wreal[:, None] * jnp.cos(phi) - wimag[:, None] * jnp.sin(phi)
        bottom = -(wimag[:, None] * jnp.cos(phi) + wreal[:, None] * jnp.sin(phi))
        col_table = jnp.concatenate([top, bottom], 0).astype(jnp.bfloat16)
        total = total + jnp.dot(row_table, col_table, preferred_element_type=jnp.float32)
    tapered = total * taper_line(R)[:, None] * taper_line(C)[None, :]
    image = fold_rows(fold_columns(tapered))
    return image


def solution(mesh):
    return jax.shard_map(
        shards,
        mesh=mesh,
        in_specs=(
            P(None, ("frow", "fcol")),
            P(None, ("frow", "fcol")),
            P(("frow", "fcol")),
            P(),
            P(),
            P("frow", "fcol", None, None),
            P(),
        ),
        out_specs=P("frow", "fcol"),
        check_vma=False,
    )
```

profile of v0, /device:TPU:71, one launch (start us, length us, event | category | flops | bytes accessed | tf_op | source)
XLA Modules:
  0.0 365.5 jit_solution(12329082438858966034)
XLA Ops:
  0.0 0.0 copy-start
  0.0 1.5 fusion.84
  4.0 0.7 broadcast_select_fusion
  4.7 105.5 %all-reduce = (s32[3,256]{1,0:T(4,128)S(1)}, s32[3,256]{1,0:T(4,128)S(1)}, s32[3,256]{1,0:T(4,128)S(1)}, s32[3,256]{1,0:T(4,128)S(1)}) all-reduce(s32[3,256]{1,0:T(4,128)S(1)} %get-tuple-element.78, s32[3,256]{1,0:T(4,128)S(1)} %get-tuple-element.76, ...), channel_id=1, replica_groups=mesh['frow'=16,'fcol'=32] {'frow','fcol'}, use_global_device_ids=true, to_apply=%region_0.1 | all-reduce | flops 3072 | bytes 24576 | tf_op jit(solution)/shard_map/psum | solution.py:29
  110.3 1.0 fusion.79
  111.3 1.7 gather_fusion.10
  113.0 1.7 gather_fusion.11
  114.8 1.7 gather_fusion.12
  116.5 1.7 gather_fusion.13
  118.2 1.7 gather_fusion.2
  120.0 1.7 gather_fusion.4
  121.7 1.7 gather_fusion.3
  123.4 1.7 gather_fusion.5
  125.2 1.7 gather_fusion.26
  126.9 1.7 gather_fusion.28
  128.7 1.7 gather_fusion.27
  130.4 1.7 gather_fusion.29
  132.1 1.7 gather_fusion.18
  133.9 1.7 gather_fusion.20
  135.6 1.7 gather_fusion.19
  137.4 1.7 gather_fusion.21
  139.1 0.0 copy-start.1
  139.1 0.0 copy-done
  139.1 1.9 gather_fusion.6
  141.1 1.9 gather_fusion.7
  143.0 1.9 gather_fusion
  145.0 1.9 gather_fusion.1
  147.0 1.9 gather_fusion.22
  148.9 1.9 gather_fusion.16
  150.9 1.9 gather_fusion.23
  152.8 1.9 gather_fusion.17
  154.8 1.9 gather_fusion.14
  156.8 1.9 gather_fusion.8
  158.7 1.9 gather_fusion.15
  160.7 1.9 gather_fusion.9
  162.6 1.9 gather_fusion.30
  164.6 1.9 gather_fusion.24
  166.6 0.0 copy-start.3
  166.6 1.9 gather_fusion.31
  168.5 1.9 gather_fusion.25
  170.6 99.6 %all-reduce.1 = (f32[2,256]{1,0:T(2,128)S(1)}, f32[2,256]{1,0:T(2,128)S(1)}, f32[2,256]{1,0:T(2,128)S(1)}, f32[2,256]{1,0:T(2,128)S(1)}) all-reduce(f32[2,256]{1,0:T(2,128)S(1)} %get-tuple-element.89, f32[2,256]{1,0:T(2,128)S(1)} %get-tuple-element.88, ...), channel_id=1, replica_groups=mesh['frow'=16,'fcol'=32] {'frow','fcol'}, use_global_device_ids=true, to_apply=%region_1.2 | all-reduce | flops 2048 | bytes 16384 | tf_op jit(solution)/shard_map/psum | solution.py:29
  270.5 19.1 %cosine_convert_fusion = (bf16[1152,256]{1,0:T(8,128)(2,1)S(1)}, bf16[1152,256]{1,0:T(8,128)(2,1)S(1)}, bf16[1152,256]{1,0:T(8,128)(2,1)S(1)}, bf16[1152,256]{1,...) fusion(s32[1152]{0:T(1024)S(1)} %add_select_fusion.8, ...), kind=kLoop, calls=%fused_computation.97 | loop fusion | flops 18874368 | bytes 4727296 | tf_op jit(solution)/shard_map/convert.2
  289.6 11.5 %subtract_convert_fusion = (bf16[256,640]{1,0:T(8,128)(2,1)S(1)}, bf16[256,640]{1,0:T(8,128)(2,1)S(1)}, bf16[256,640]{1,0:T(8,128)(2,1)S(1)}, bf16[256,640]{1,0:...) fusion(f32[256]{0:T(256)S(1)} %add_multiply_fusion, ...), kind=kLoop, calls=%fused_computation.137 | loop fusion | flops 15073280 | bytes 2636288 | tf_op jit(solution)/shard_map/convert
  301.0 1.1 fusion.14
  302.1 1.1 convolution_add_fusion.2
  303.2 1.1 convolution_add_fusion.1
  304.3 1.2 fusion.1
  305.5 6.8 %collective-permute-start = (f32[1152,64]{0,1:T(8,128)S(1)}, f32[1152,64]{0,1:T(8,128)S(1)}, u32[]{:S(2)}, u32[]{:S(2)}) collective-permute-start(f32[1152,64]{0,1:T(8,128)S(1)} %slice.281), channel_id=1, source_target_pairs={{0,1},{1,2},{2,3},{3,4},{4,5},{5,6},{6,7},{7,8},{8,9},{9,10},{10,1... | collective-permute-start | bytes 884744 | tf_op jit(solution)/shard_map/ppermute | solution.py:21
  312.3 10.0 %collective-permute-done = f32[1152,64]{0,1:T(8,128)S(1)} collective-permute-done((f32[1152,64]{0,1:T(8,128)S(1)}, f32[1152,64]{0,1:T(8,128)S(1)}, u32[]{:S(2)}, u32[]{:S(2)}) %collective-permute-start) | collective-permute-done | bytes 294944 | tf_op jit(solution)/shard_map/ppermute | solution.py:21
  322.4 1.9 collective-permute-start.1
  324.3 0.1 slice.282
  324.4 20.4 %collective-permute-done.1 = f32[1152,64]{0,1:T(8,128)S(1)} collective-permute-done((f32[1152,64]{0,1:T(8,128)S(1)}, f32[1152,64]{0,1:T(8,128)S(1)}, u32[]{:S(2)}, u32[]{:S(2)}) %collective-permute-start.1) | collective-permute-done | bytes 294944 | tf_op jit(solution)/shard_map/ppermute | solution.py:22
  344.9 0.1 pad_maximum_fusion.3
  345.1 1.9 collective-permute-start.2
  347.0 7.3 %collective-permute-done.2 = f32[64,512]{0,1:T(8,128)S(1)} collective-permute-done((f32[64,512]{0,1:T(8,128)S(1)}, f32[64,512]{0,1:T(8,128)S(1)}, u32[]{:S(2)}, u32[]{:S(2)}) %collective-permute-start.2) | collective-permute-done | bytes 131104 | tf_op jit(solution)/shard_map/ppermute | solution.py:21
  354.3 0.1 maximum_add_fusion.1
  354.4 1.9 collective-permute-start.3
  356.4 0.2 pad_maximum_fusion
  356.5 0.0 copy-start.2
  356.5 1.4 copy-done.2
  358.0 3.6 collective-permute-done.3
  361.6 1.5 slice-done
  363.0 0.7 pad_maximum_fusion.1
  363.7 1.8 copy.9
  (48 shorter events, 0.5 us)
Async XLA Ops:
  0.0 139.1 %copy-start = (s32[512]{0:T(512)S(1)}, s32[512]{0:T(512)}, u32[]{:S(2)}) copy-start(s32[512]{0:T(512)} %param.11) | copy-start | bytes 6148
  139.1 4.0 %copy-start.1 = (s32[512]{0:T(512)S(1)}, s32[512]{0:T(512)}, u32[]{:S(2)}) copy-start(s32[512]{0:T(512)} %param.10) | copy-start | bytes 6148
  166.6 4.0 %copy-start.3 = (f32[2,256]{1,0:T(2,128)S(1)}, f32[2,256]{1,0:T(2,128)}, u32[]{:S(2)}) copy-start(f32[2,256]{1,0:T(2,128)} %param.7) | copy-start | bytes 6148
  305.5 16.8 %collective-permute-start = (f32[1152,64]{0,1:T(8,128)S(1)}, f32[1152,64]{0,1:T(8,128)S(1)}, u32[]{:S(2)}, u32[]{:S(2)}) collective-permute-start(f32[1152,64]{0,1:T(8,128)S(1)} %slice.281), channel_id=1, source_target_pairs={{0,1},{1,2},{2,3},{3,4},{4,5},{5,6},{6,7},{7,8},{8,9},{9,10},{10,1... | collective-permute-start | bytes 884744 | tf_op jit(solution)/shard_map/ppermute | solution.py:21
  322.4 22.5 %collective-permute-start.1 = (f32[1152,64]{0,1:T(8,128)S(1)}, f32[1152,64]{0,1:T(8,128)S(1)}, u32[]{:S(2)}, u32[]{:S(2)}) collective-permute-start(f32[1152,64]{0,1:T(8,128)S(1)} %get-tuple-element.26), channel_id=1, source_target_pairs={{1,0},{2,1},{3,2},{4,3},{5,4},{6,5},{7,6},{8,7},{9,8},{10,9},{11,1... | collective-permute-start | bytes 884744 | tf_op jit(solution)/shard_map/ppermute | solution.py:22
  345.1 9.2 %collective-permute-start.2 = (f32[64,512]{0,1:T(8,128)S(1)}, f32[64,512]{0,1:T(8,128)S(1)}, u32[]{:S(2)}, u32[]{:S(2)}) collective-permute-start(f32[64,512]{0,1:T(8,128)S(1)} %pad_maximum_fusion.3), channel_id=1, source_target_pairs={{0,32},{32,64},{64,96},{96,128},{128,160},{160,192},{192,224},{224... | collective-permute-start | bytes 393224 | tf_op jit(solution)/shard_map/ppermute | solution.py:21
  354.4 7.1 %collective-permute-start.3 = (f32[64,512]{0,1:T(8,128)S(1)}, f32[64,512]{0,1:T(8,128)S(1)}, u32[]{:S(2)}, u32[]{:S(2)}) collective-permute-start(f32[64,512]{0,1:T(8,128)S(1)} %get-tuple-element.28), channel_id=1, source_target_pairs={{32,0},{64,32},{96,64},{128,96},{160,128},{192,160},{224,192},{256... | collective-permute-start | bytes 393224 | tf_op jit(solution)/shard_map/ppermute | solution.py:22
  356.5 1.4 copy-start.2
  361.5 1.5 slice-start
where the time goes:
time: 366 us
  blocking collectives  205 us (56%)
  local copies, waits for them, and re-layouts  66 us (18%)
  waiting for transfers between devices  41.3 us (11%)
  other arithmetic  32.8 us (9%)
  starting transfers between devices  12.6 us (3%)
  matrix products  4.44 us (1%)
    psum x2, blocking collectives, broadcast(): return lax.psum(kept, axis)  205 us
    another operation x2, other arithmetic  30.5 us
    ppermute x2, waiting for transfers between devices, extended_2(): after = lax.ppermute(leading, axis, down)  24 us
    ppermute x2, waiting for transfers between devices, extended_2(): before = lax.ppermute(last, axis, up)  17.3 us
    gather x8, local copies, waits for them, and re-layouts, shards(): frequency_v = station_v_cells[tag_names[0]] - station_v_cells[tag_names[1]]  15.6 us
    gather x8, local copies, waits for them, and re-layouts, shards(): frequency_u = station_u_cells[tag_names[0]] - station_u_cells[tag_names[1]]  15.6 us
    ppermute x2, starting transfers between devices, extended_2(): before = lax.ppermute(last, axis, up)  8.72 us
  transfers between devices with their start and end apart: 4, of which 4 were waited for; matrix products, arithmetic and copies ran while one was open for 0% of the time, Pallas kernels for 0%

commit v1 on v0

--- a/solution.py
+++ b/solution.py
@@ -26,7 +26,7 @@
 
 def broadcast(value, axis, source):
     kept = jnp.where(lax.axis_index(axis) == source, value, 0).astype(value.dtype)
-    return lax.psum(kept, axis)
+    return jnp.sum(lax.all_gather(kept, axis), axis=0)
 
 
 def taper_line(length):

time: 366 us -> 6250 us (17.08)
  waiting for transfers between devices: 41.3 us -> 6100 us
  blocking collectives: 205 us -> 0 us
    all_gather x0 -> x8, waiting for transfers between devices: none -> 6050 us  [broadcast(): return jnp.sum(lax.all_gather(kept, axis), axis=0)]
    psum x2 -> x0, blocking collectives: 205 us -> none  [broadcast(): return lax.psum(kept, axis)]
  transfers between devices with their start and end apart: 4 -> 12, of which waited for: 4 -> 12; matrix products, arithmetic and copies ran while one was open for 0% -> 1% of each run, Pallas kernels for 0% -> 0%
where the time goes in v1:
time: 6250 us
  waiting for transfers between devices  6100 us (98%)
  local copies, waits for them, and re-layouts  66.4 us (1%)
    all_gather x8, waiting for transfers between devices, broadcast(): return jnp.sum(lax.all_gather(kept, axis), axis=0)  6050 us
  transfers between devices with their start and end apart: 12, of which 12 were waited for; matrix products, arithmetic and copies ran while one was open for 1% of the time, Pallas kernels for 0%

profile of v1, /device:TPU:71, one launch (start us, length us, event | category | flops | bytes accessed | tf_op | source)
XLA Modules:
  0.0 6250.2 jit_solution(1130338181479251925)
XLA Ops:
  6.5 1.5 fusion.81
  10.6 1.3 select_bitcast_fusion
  14.0 1.3 broadcast_select_fusion
  18.5 760.6 %all-gather.29.cloned.1.call-done = f32[512,2,256]{2,1,0:T(2,128)} async-done(((f32[1,2,256]{2,1,0:T(2,128)}), f32[512,2,256]{2,1,0:T(2,128)}) %all-gather.29.cloned.1.call-update) | async-done | bytes 1048592 | tf_op jit(solution)/shard_map/all_gather | solution.py:29
  779.1 1.8 reduce_sum.77
  780.9 758.4 %all-gather.31.cloned.1.call-done = f32[512,2,256]{2,1,0:T(2,128)} async-done(((f32[1,2,256]{2,1,0:T(2,128)}), f32[512,2,256]{2,1,0:T(2,128)}) %all-gather.31.cloned.1.call-update) | async-done | bytes 1048592 | tf_op jit(solution)/shard_map/all_gather | solution.py:29
  1539.2 1.8 reduce_sum.79
  1541.0 758.4 %all-gather.27.cloned.1.call-done = f32[512,2,256]{2,1,0:T(2,128)} async-done(((f32[1,2,256]{2,1,0:T(2,128)}), f32[512,2,256]{2,1,0:T(2,128)}) %all-gather.27.cloned.1.call-update) | async-done | bytes 1048592 | tf_op jit(solution)/shard_map/all_gather | solution.py:29
  2299.4 1.8 reduce_sum.75
  2301.2 758.2 %all-gather.25.cloned.1.call-done = f32[512,2,256]{2,1,0:T(2,128)} async-done(((f32[1,2,256]{2,1,0:T(2,128)}), f32[512,2,256]{2,1,0:T(2,128)}) %all-gather.25.cloned.1.call-update) | async-done | bytes 1048592 | tf_op jit(solution)/shard_map/all_gather | solution.py:29
  3059.4 1.8 reduce_sum.73
  3061.3 760.2 %all-gather.21.cloned.1.call-done = s32[512,3,256]{2,1,0:T(4,128)} async-done(((s32[1,3,256]{2,1,0:T(4,128)}), s32[512,3,256]{2,1,0:T(4,128)}) %all-gather.21.cloned.1.call-update) | async-done | bytes 1572880 | tf_op jit(solution)/shard_map/all_gather | solution.py:29
  3821.5 2.1 reduce_sum.76
  3823.6 1.9 gather_fusion.18
  3825.5 1.7 gather_fusion.19
  3827.3 1.7 gather_fusion.20
  3829.0 1.7 gather_fusion.21
  3830.7 752.7 %all-gather.23.cloned.1.call-done = s32[512,3,256]{2,1,0:T(4,128)} async-done(((s32[1,3,256]{2,1,0:T(4,128)}), s32[512,3,256]{2,1,0:T(4,128)}) %all-gather.23.cloned.1.call-update) | async-done | bytes 1572880 | tf_op jit(solution)/shard_map/all_gather | solution.py:29
  4583.4 2.1 reduce_sum.78
  4585.6 1.7 gather_fusion.26
  4587.3 1.7 gather_fusion.28
  4589.0 1.7 gather_fusion.27
  4590.8 1.7 gather_fusion.29
  4592.5 753.0 %all-gather.19.cloned.1.call-done = s32[512,3,256]{2,1,0:T(4,128)} async-done(((s32[1,3,256]{2,1,0:T(4,128)}), s32[512,3,256]{2,1,0:T(4,128)}) %all-gather.19.cloned.1.call-update) | async-done | bytes 1572880 | tf_op jit(solution)/shard_map/all_gather | solution.py:29
  5345.5 2.1 reduce_sum.74
  5347.7 1.7 gather_fusion.10
  5349.4 1.7 gather_fusion.12
  5351.1 1.7 gather_fusion.11
  5352.9 1.7 gather_fusion.13
  5354.6 753.0 %all-gather.17.cloned.1.call-done = s32[512,3,256]{2,1,0:T(4,128)} async-done(((s32[1,3,256]{2,1,0:T(4,128)}), s32[512,3,256]{2,1,0:T(4,128)}) %all-gather.17.cloned.1.call-update) | async-done | bytes 1572880 | tf_op jit(solution)/shard_map/all_gather | solution.py:29
  6107.6 2.1 reduce_sum.72
  6109.8 1.7 gather_fusion.2
  6111.5 1.7 gather_fusion.4
  6113.2 1.7 gather_fusion.3
  6115.0 1.7 gather_fusion.5
  6116.7 1.9 gather_fusion.6
  6118.7 1.9 gather_fusion.7
  6120.7 1.9 gather_fusion
  6122.6 1.9 gather_fusion.1
  6124.6 1.9 gather_fusion.14
  6126.5 1.9 gather_fusion.8
  6128.5 1.9 gather_fusion.15
  6130.4 1.9 gather_fusion.9
  6132.4 1.9 gather_fusion.22
  6134.4 1.9 gather_fusion.16
  6136.3 1.9 gather_fusion.23
  6138.3 1.9 gather_fusion.17
  6140.3 1.9 gather_fusion.30
  6142.2 1.9 gather_fusion.24
  6144.2 2.2 gather_fusion.31
  6146.3 1.9 gather_fusion.25
  6148.5 19.1 cosine_convert_fusion
  6167.6 11.5 subtract_convert_fusion
  6183.5 8.2 collective-permute-start
  6191.8 10.1 collective-permute-done
  6201.9 1.9 collective-permute-start.1
  6204.0 18.8 collective-permute-done.1
  6222.9 1.9 collective-permute-start.2
  6224.8 7.3 collective-permute-done.2
  6232.3 1.9 collective-permute-start.3
  6234.4 1.4 copy-done.2
  6235.8 3.6 collective-permute-done.3
  6239.4 1.5 slice-done
  6241.6 1.8 copy.10
  (74 shorter events, 11.2 us)
Async XLA Ops:
  6.5 6110.2 %copy-start = (s32[512]{0:T(512)S(1)}, s32[512]{0:T(512)}, u32[]{:S(2)}) copy-start(s32[512]{0:T(512)} %param.11) | copy-start | bytes 6148
  6.5 772.5 %all-gather.29.cloned.1.call-start = ((), (), s32[]{:S(2)}) async-start(), calls=%async_computation.6 | async-start | bytes 1050624 | tf_op jit(solution)/shard_map/all_gather | solution.py:29
  11.9 1527.3 %all-gather.31.cloned.1.call-start = ((), (), s32[]{:S(2)}) async-start(), calls=%async_computation.7 | async-start | bytes 1050624 | tf_op jit(solution)/shard_map/all_gather | solution.py:29
  12.6 2286.8 %all-gather.27.cloned.1.call-start = ((), (), s32[]{:S(2)}) async-start(), calls=%async_computation.5 | async-start | bytes 1050624 | tf_op jit(solution)/shard_map/all_gather | solution.py:29
  13.4 3046.1 %all-gather.25.cloned.1.call-start = ((), (), s32[]{:S(2)}) async-start(), calls=%async_computation.4 | async-start | bytes 1050624 | tf_op jit(solution)/shard_map/all_gather | solution.py:29
  14.0 3807.5 %all-gather.21.cloned.1.call-start = ((), (), s32[]{:S(2)}) async-start(), calls=%async_computation.2 | async-start | bytes 2101248 | tf_op jit(solution)/shard_map/all_gather | solution.py:29
  15.3 4568.1 %all-gather.23.cloned.1.call-start = ((), (), s32[]{:S(2)}) async-start(), calls=%async_computation.3 | async-start | bytes 2101248 | tf_op jit(solution)/shard_map/all_gather | solution.py:29
  15.9 5329.6 %all-gather.19.cloned.1.call-start = ((), (), s32[]{:S(2)}) async-start(), calls=%async_computation.1 | async-start | bytes 2101248 | tf_op jit(solution)/shard_map/all_gather | solution.py:29
  16.7 6090.9 %all-gather.17.cloned.1.call-start = ((), (), s32[]{:S(2)}) async-start(), calls=%async_computation | async-start | bytes 2101248 | tf_op jit(solution)/shard_map/all_gather | solution.py:29
  6116.7 4.0 copy-start.1
  6183.5 18.3 collective-permute-start
  6201.9 20.8 collective-permute-start.1
  6222.9 9.2 collective-permute-start.2
  6232.3 7.1 collective-permute-start.3
  6234.4 1.4 copy-start.2
  6239.4 1.5 slice-start
Sparse Core Ops, SparseCore 0:
  12.0 767.0 all-gather.28
  781.2 758.0 all-gather.30
  1541.4 758.0 all-gather.26
  2301.4 758.0 all-gather.24
  3061.4 759.9 all-gather.20
  3823.4 759.9 all-gather.22
  4585.5 759.9 all-gather.18
  5347.6 759.9 all-gather.16
